TPU v7x, 32 devices: a whole 2x2x4 slice. The times are simulated.
32 devices in a mesh: boot: 4 (over z), tm: 8 (over y, x, core).
Axes of the slice: x: 2, y: 2, z: 4, core: 2. Of those that a mesh axis runs over, the one named last changes fastest.
Arguments:
- recording: bfloat16 [4096, 1024], P('tm'), may hold values from -60 to 60, as said below
- starts: int32 [4, 48], P('boot', 'tm'), may hold values from 0 to 448, as said below
- lengths: int32 [4, 48], P('boot', 'tm'), may hold values from 1 to 64, as said below
- support: int32 [4, 4096], P(None, 'boot'), may hold values 0 or 1
Outputs:
- averaged: float32 [32, 4096], P(None, 'boot')
- residual: float32 [32, 4096], P(None, 'tm')
Inputs may be any that keep to these rules, and one draw needn't show every extreme that they name: A shard's values are an autoregressive recording; its values stay within the range. Entry [b, j * 6 + k] starts block k of resample b on time shard j, counted from the shard's first sample; a block ends inside its shard. The 6 lengths of one resample on one time shard sum to at most 384.
All inputs are finite; a program needn't handle non-finite values. No bound on the sum of `support` on one device may be relied on, other than what follows from the above.
Results may differ from a plain program's by a relative error of at most 0.0043.
The roundings to bfloat16 on the way count: a program that leaves them out, or rounds other values in their place, can miss the bound.
Values may be sent and summed in bfloat16 or wider, within the bound.
No kernel may reach another device: no remote copies, remote signals or barrier semaphores. Data moves between devices by JAX's collectives and lax.ppermute only.
A program may use at most 64 MiB of HBM per device.

v0:
```python
import jax
import jax.numpy as jnp
from jax import lax
from jax.sharding import PartitionSpec as P

CHANNEL_COUNT = 1024
LAGS = 4
RESPONSE_COUNT = 32
NBLK = 6
CAP = 384
ITERS = 3
CHEB = 5
ridge_weight = 4.0
shrink_level = 0.75
epsilon = 1e-05


def passed_along(block, axis, distance):
    devices = range(lax.axis_size(axis))
    route = [(i - distance, i) for i in devices if i - distance in devices]
    return lax.ppermute(block, axis, route)


def bootstrap_rows(window, begins, sizes):
    ends = jnp.cumsum(sizes)
    offsets = ends - sizes
    total = ends[-1]
    rows = jnp.arange(CAP, dtype=jnp.int32)
    member = (rows[:, None] >= offsets[None, :]).astype(jnp.int32)
    which = jnp.sum(member, axis=1) - 1
    picked = (which[:, None] == jnp.arange(NBLK, dtype=jnp.int32)[None, :]).astype(jnp.int32)
    anchor = jnp.sum(picked * offsets[None, :], axis=1)
    opening = jnp.sum(picked * begins[None, :], axis=1)
    live = rows < total
    times = jnp.where(live, opening + rows - anchor, 0)
    blocks = [jnp.take(window, times + LAGS - 1 - delay_step, axis=0) for delay_step in range(LAGS)]
    design = jnp.concatenate(blocks, axis=1)
    design = jnp.where(live[:, None], design, jnp.zeros_like(design))
    answer = jnp.take(window[:, :RESPONSE_COUNT], times + LAGS, axis=0)
    answer = jnp.where(live[:, None], answer, jnp.zeros_like(answer))
    return (design, answer.T)


def chebyshev(gram, rhs, bound):
    center = ridge_weight + 0.5 * bound
    radius = 0.5 * bound
    sigma = center / radius
    solution = jnp.zeros_like(rhs)
    remain = rhs
    factor = 1.0 / sigma
    update = rhs / center
    for count in range(CHEB):
        solution = solution + update
        if count + 1 < CHEB:
            applied = ridge_weight * update + jnp.einsum(
                "brc,bcd->brd", update, gram, precision=lax.Precision.HIGHEST
            )
            remain = remain - applied
            after = 1.0 / (2.0 * sigma - factor)
            update = after * factor * update + 2.0 * after / radius * remain
            factor = after
    return solution


def shrink_columns(mean_value, norms, level):
    return mean_value * (jnp.maximum(norms - level, 0.0) / jnp.maximum(norms, level))[:, None, :]


def per_device(recording, starts, lengths, support):
    shards = lax.axis_size("tm")
    samples = recording.shape[0]
    values = recording.astype(jnp.float32)
    power = lax.psum(jnp.sum(values * values, axis=0), "tm")
    scale = 1.0 / jnp.sqrt(power / (samples * shards) + epsilon)
    scaled_input = (values * scale).astype(jnp.bfloat16)
    carried = passed_along(scaled_input[samples - LAGS :], "tm", 1)
    extended = jnp.concatenate([carried, scaled_input], axis=0)
    design, answer = jax.vmap(bootstrap_rows, in_axes=(None, 0, 0))(extended, starts, lengths)
    row_scale = 1.0 / CAP
    cross = (
        jnp.einsum("brc,bcf->brf", answer, design, preferred_element_type=jnp.float32) * row_scale
    )
    gram = (
        jnp.einsum("bcf,bdf->bcd", design, design, preferred_element_type=jnp.float32) * row_scale
    )
    bound = jnp.sqrt(jnp.sum(gram * gram, axis=(1, 2)))[:, None, None]
    consensus = jnp.zeros_like(cross)
    dual = jnp.zeros_like(cross)
    for rounds in range(ITERS):
        target = cross + ridge_weight * (consensus - dual)
        projected = (
            jnp.einsum(
                "brf,bcf->brc",
                target.astype(jnp.bfloat16),
                design,
                preferred_element_type=jnp.float32,
            )
            * row_scale
        )
        weights = chebyshev(gram, projected, bound)
        back = jnp.einsum(
            "brc,bcf->brf", weights.astype(jnp.bfloat16), design, preferred_element_type=jnp.float32
        )
        local = (target - back) / ridge_weight
        stacked = local + dual
        mean_value = lax.psum(stacked, "tm") / shards
        norms = jnp.sqrt(jnp.sum(mean_value * mean_value, axis=1))
        level = shrink_level * jnp.mean(norms, axis=1, keepdims=True)
        consensus = shrink_columns(mean_value, norms, level)
        dual = dual + local - consensus
    width = consensus.shape[2] // lax.axis_size("boot")
    position = lax.axis_index("boot")
    chosen = support.astype(jnp.float32)
    tally = jnp.sum(chosen, axis=0)
    mine = lax.all_to_all(support, "boot", split_axis=0, concat_axis=1, tiled=True).astype(
        jnp.float32
    )
    weighted = jnp.sum(mine[:, None, :] * consensus, axis=0)
    summed = lax.psum_scatter(weighted, "boot", scatter_dimension=1, tiled=True)
    averaged = summed / jnp.maximum(tally, 1.0)[None, :]
    opening = position * width
    delay_step = opening // CHANNEL_COUNT
    channel = opening % CHANNEL_COUNT
    columns = lax.dynamic_slice(extended, (LAGS - 1 - delay_step, channel), (samples, width))
    partial_result = lax.dot_general(
        averaged.astype(jnp.bfloat16),
        columns,
        (((1,), (1,)), ((), ())),
        preferred_element_type=jnp.float32,
    )
    predicted_output = lax.psum(partial_result, "boot")
    residual = scaled_input[:, :RESPONSE_COUNT].astype(jnp.float32).T - predicted_output
    return (averaged, residual)


def solution(mesh):
    in_specs = (P("tm", None), P("boot", "tm"), P("boot", "tm"), P(None, "boot"))
    out_specs = (P(None, "boot"), P(None, "tm"))
    return jax.shard_map(
        per_device, mesh=mesh, in_specs=in_specs, out_specs=out_specs, check_vma=False
    )
```

profile of v0, /device:TPU:0, one launch (start us, length us, event | category | flops | bytes accessed | tf_op | source)
XLA Modules:
  0.0 315.7 jit_solution(589085711330140276)
XLA Ops:
  7.2 1.5 copy.24
  9.0 15.2 %psum.35 = f32[1024]{0:T(1024)S(1)} all-reduce(f32[1024]{0:T(1024)S(1)} %fusion.9), channel_id=1, replica_groups=mesh['boot'=4,'tm'=8] {'tm'}, use_global_device_ids=true, to_apply=%region_5.6 | all-reduce | flops 1024 | bytes 8192 | tf_op jit(solution)/shard_map/psum | solution.py:73
  24.6 1.3 collective-permute-start
  26.1 0.6 slice.12
  26.9 0.7 iota_compare_fusion
  27.6 0.7 fusion.114
  28.3 0.7 and_reduce_fusion.3
  29.1 0.7 copy-done.10
  29.8 0.7 pad_maximum_fusion
  30.5 0.6 copy.26
  31.1 2.7 gather_fusion.4
  33.8 2.7 gather_fusion.3
  36.5 2.7 gather_fusion.2
  39.2 2.7 gather_fusion.1
  41.9 2.7 fusion.38
  44.5 1.4 fusion.42
  45.9 0.9 fusion.8
  46.8 2.5 multiply_reduce_fusion
  50.7 1.4 gather_fusion
  52.1 2.7 convolution_multiply_fusion
  54.8 2.1 maximum_select_fusion.1
  56.9 1.0 convolution_multiply_fusion.4
  58.8 0.4 fusion.29
  59.3 0.4 fusion.32
  59.7 1.5 fusion.1
  61.5 58.2 %all-reduce.5.cloned.1.call-done = f32[1,32,4096]{2,1,0:T(8,128)} async-done(((f32[1,32,4096]{2,1,0:T(8,128)}), f32[1,32,4096]{2,1,0:T(8,128)}) %all-reduce.5.cloned.1.call-update) | async-done | bytes 524304 | tf_op jit(solution)/shard_map/psum | solution.py:106
  119.7 1.1 multiply_reduce_fusion.3
  120.8 0.7 sqrt_reduce_fusion.2
  122.1 3.4 %convolution_multiply_fusion.3 = f32[32,384]{1,0:T(8,128)S(1)} fusion(bf16[384,4096]{1,0:T(8,128)(2,1)} %copy-done.3, f32[1,32,4096]{2,1,0:T(8,128)} %fusion.1, f32[1,32,4096]{2,1,0:T(8,128)} %all-reduce.5.cloned.1.call-done, f32[32,4096]{1,0:T(8,128)S(1)} %convolution_multiply_fusion, f32[4096]{0:T(1024)S(1)} %divide_multiply_fusion.2), kind=kOutput, calls=%fused_computation.31 | convolution fusion | flops 101462016 | bytes 4784128 | tf_op jit(solution)/shard_map/brf,bcf->brc/dot_general | solution.py:92
  126.8 0.4 fusion.33
  127.3 1.5 fusion.7
  129.0 54.2 %all-reduce.7.cloned.1.call-done = f32[1,32,4096]{2,1,0:T(8,128)} async-done(((f32[1,32,4096]{2,1,0:T(8,128)}), f32[1,32,4096]{2,1,0:T(8,128)}) %all-reduce.7.cloned.1.call-update) | async-done | bytes 524304 | tf_op jit(solution)/shard_map/psum | solution.py:106
  183.2 1.1 multiply_reduce_fusion.2
  184.3 0.7 sqrt_reduce_fusion.1
  185.6 3.4 %convolution_multiply_fusion.2 = f32[32,384]{1,0:T(8,128)S(1)} fusion(bf16[384,4096]{1,0:T(8,128)(2,1)} %copy-done.3, f32[1,32,4096]{2,1,0:T(8,128)} %fusion.7, f32[1,32,4096]{2,1,0:T(8,128)} %all-reduce.7.cloned.1.call-done, f32[32,4096]{1,0:T(8,128)S(1)} %convolution_multiply_fusion, f32[4096]{0:T(1024)S(1)} %divide_multiply_fusion.1), kind=kOutput, calls=%fused_computation.30 | convolution fusion | flops 101462016 | bytes 4784128 | tf_op jit(solution)/shard_map/brf,bcf->brc/dot_general | solution.py:92
  189.9 0.4 fusion.15
  190.4 0.4 fusion.34
  190.9 1.5 fusion.4
  192.5 9.9 %all_to_all.13 = s32[4,1,1024]{2,1,0:T(1,128)S(1)} all-to-all(s32[4,1,1024]{2,1,0:T(1,128)S(1)} %all_to_all.10), channel_id=1, replica_groups=mesh['boot'=4,'tm'=8] {'boot'}, dimensions={0} | all-to-all | bytes 32768 | tf_op jit(solution)/shard_map/all_to_all | solution.py:115
  202.5 44.2 %all-reduce.9.cloned.1.call-done = f32[1,32,4096]{2,1,0:T(8,128)} async-done(((f32[1,32,4096]{2,1,0:T(8,128)}), f32[1,32,4096]{2,1,0:T(8,128)}) %all-reduce.9.cloned.1.call-update) | async-done | bytes 524304 | tf_op jit(solution)/shard_map/psum | solution.py:106
  246.7 1.1 multiply_reduce_fusion.1
  247.8 0.6 sqrt_reduce_fusion
  249.1 1.9 multiply_bitcast_fusion
  251.1 21.2 %reduce-scatter.2.cloned.1.call-done = f32[32,1024]{1,0:T(8,128)} async-done(((f32[32,4096]{1,0:T(8,128)}), f32[32,1024]{1,0:T(8,128)}) %reduce-scatter.2.cloned.1.call-update) | async-done | bytes 131088 | tf_op jit(solution)/shard_map/reduce_scatter | solution.py:119
  272.4 0.9 broadcast_divide_fusion
  273.3 1.3 fusion.36
  274.6 33.1 %all-reduce.11.cloned.1.call-done = f32[32,512]{1,0:T(8,128)} async-done(((f32[32,512]{1,0:T(8,128)}), f32[32,512]{1,0:T(8,128)}) %all-reduce.11.cloned.1.call-update) | async-done | bytes 65552 | tf_op jit(solution)/shard_map/psum | solution.py:131
  307.7 1.5 bitcast_subtract_fusion
  (73 shorter events, 5.0 us)
Async XLA Ops:
  7.2 18.8 %copy-start.15 = (s32[1,6]{1,0:T(1,128)S(1)}, s32[1,6]{1,0:T(1,128)}, u32[]{:S(2)}) copy-start(s32[1,6]{1,0:T(1,128)} %param.8) | copy-start | bytes 76
  7.2 19.6 %copy-start.14 = (s32[1,6]{1,0:T(1,128)S(1)}, s32[1,6]{1,0:T(1,128)}, u32[]{:S(2)}) copy-start(s32[1,6]{1,0:T(1,128)} %param.7) | copy-start | bytes 76
  7.2 112.5 %all-reduce.5.cloned.1.call-start = ((), (), s32[]{:S(2)}) async-start(), calls=%async_computation.2 | async-start | bytes 1048576 | tf_op jit(solution)/shard_map/psum | solution.py:106
  24.6 4.4 %collective-permute-start = (bf16[4,1024]{0,1:T(8,128)(2,1)S(1)}, bf16[4,1024]{0,1:T(8,128)(2,1)S(1)}, u32[]{:S(2)}, u32[]{:S(2)}) collective-permute-start(bf16[4,1024]{0,1:T(8,128)(2,1)S(1)} %slice.26), channel_id=1, source_target_pairs={{0,1},{1,2},{2,3},{3,4},{4,5},{5,6},{6,7},{8,9},{9,10},{10,11},{11... | collective-permute-start | bytes 24584 | tf_op jit(solution)/shard_map/ppermute | solution.py:21
  29.1 0.7 copy-start.10
  41.9 2.7 copy-start.8
  41.9 2.7 copy-start.9
  46.8 2.5 copy-start.3
  46.8 3.4 %copy-start.11 = (bf16[4,1024]{0,1:T(8,128)(2,1)S(1)}, bf16[4,1024]{0,1:T(8,128)(2,1)}, u32[]{:S(2)}) copy-start(bf16[4,1024]{0,1:T(8,128)(2,1)} %copy-done.10) | copy-start | bytes 24580
  56.9 2.8 copy-start
  61.3 121.9 %all-reduce.7.cloned.1.call-start = ((), (), s32[]{:S(2)}) async-start(), calls=%async_computation.3 | async-start | bytes 1048576 | tf_op jit(solution)/shard_map/psum | solution.py:106
  122.1 5.2 %copy-start.1 = (bf16[384,4096]{1,0:T(8,128)(2,1)S(1)}, bf16[384,4096]{1,0:T(8,128)(2,1)}, u32[]{:S(2)}) copy-start(bf16[384,4096]{1,0:T(8,128)(2,1)} %copy-done) | copy-start | bytes 9437188
  122.1 5.2 %copy-start.5 = (f32[1,32,4096]{2,1,0:T(8,128)S(1)}, f32[1,32,4096]{2,1,0:T(8,128)}, u32[]{:S(2)}) copy-start(f32[1,32,4096]{2,1,0:T(8,128)} %fusion.1) | copy-start | bytes 1572868
  122.1 5.2 %copy-start.7 = (f32[1,32,4096]{2,1,0:T(8,128)S(1)}, f32[1,32,4096]{2,1,0:T(8,128)}, u32[]{:S(2)}) copy-start(f32[1,32,4096]{2,1,0:T(8,128)} %all-reduce.5.cloned.1.call-done) | copy-start | bytes 1572868
  128.9 117.8 %all-reduce.9.cloned.1.call-start = ((), (), s32[]{:S(2)}) async-start(), calls=%async_computation.4 | async-start | bytes 1048576 | tf_op jit(solution)/shard_map/psum | solution.py:106
  185.6 5.2 %copy-start.2 = (bf16[384,4096]{1,0:T(8,128)(2,1)S(1)}, bf16[384,4096]{1,0:T(8,128)(2,1)}, u32[]{:S(2)}) copy-start(bf16[384,4096]{1,0:T(8,128)(2,1)} %copy-done) | copy-start | bytes 9437188
  185.6 5.2 %copy-start.4 = (f32[1,32,4096]{2,1,0:T(8,128)S(1)}, f32[1,32,4096]{2,1,0:T(8,128)}, u32[]{:S(2)}) copy-start(f32[1,32,4096]{2,1,0:T(8,128)} %fusion.7) | copy-start | bytes 1572868
  185.6 5.2 %copy-start.6 = (f32[1,32,4096]{2,1,0:T(8,128)S(1)}, f32[1,32,4096]{2,1,0:T(8,128)}, u32[]{:S(2)}) copy-start(f32[1,32,4096]{2,1,0:T(8,128)} %all-reduce.7.cloned.1.call-done) | copy-start | bytes 1572868
  190.4 2.1 copy-start.13
  192.4 79.9 %reduce-scatter.2.cloned.1.call-start = ((), (), s32[]{:S(2)}) async-start(), calls=%async_computation.5 | async-start | bytes 655360 | tf_op jit(solution)/shard_map/reduce_scatter | solution.py:119
  251.0 56.6 %all-reduce.11.cloned.1.call-start = ((), (), s32[]{:S(2)}) async-start(), calls=%async_computation.6 | async-start | bytes 131072 | tf_op jit(solution)/shard_map/psum | solution.py:131
  273.3 35.9 %copy-start.12 = (f32[32,1024]{1,0:T(8,128)}, f32[32,1024]{1,0:T(8,128)S(1)}, u32[]{:S(2)}) copy-start(f32[32,1024]{1,0:T(8,128)S(1)} %broadcast_divide_fusion) | copy-start | bytes 393220
Sparse Core Ops, SparseCore 0:
  61.4 58.2 all-reduce.4
  129.0 54.1 all-reduce.6
  192.5 54.1 all-reduce.8
  251.2 21.1 reduce-scatter.1
  275.1 32.5 all-reduce.10
where the time goes:
time: 316 us
  waiting for transfers between devices  211 us (67%)
  blocking collectives  25.1 us (8%)
  matrix products  24 us (8%)
  other arithmetic  20.6 us (7%)
  between operations  17.4 us (6%)
  local copies, waits for them, and re-layouts  15.9 us (5%)
    psum x3, waiting for transfers between devices, per_device(): mean_value = lax.psum(stacked, 'tm') / shards  157 us
    psum x1, waiting for transfers between devices, per_device(): predicted_output = lax.psum(partial_result, 'boot')  33.1 us
    reduce_scatter x1, waiting for transfers between devices, per_device(): summed = lax.psum_scatter(weighted, 'boot', scatter_dimension=1, tiled=True)  21.2 us
    psum x1, blocking collectives, per_device(): power = lax.psum(jnp.sum(values * values, axis=0), 'tm')  15.2 us
    gather x4, local copies, waits for them, and re-layouts, bootstrap_rows(): jnp.take(window, times + LAGS - 1 - delay_step, axis=0)  10.8 us
    all_to_all x1, blocking collectives, per_device(): lax.all_to_all(support, 'boot', split_axis=0, concat_axis=1, tiled=True)  9.94 us
    dot_general x3, matrix products, per_device(): jnp.einsum('brf,bcf->brc', target.astype(jnp.bfloat16), design, preferred...  7.84 us
  transfers between devices with their start and end apart: 6, of which 5 were waited for; matrix products, arithmetic and copies ran while one was open for 1% of the time, Pallas kernels for 0%

commit v1 on v0

--- a/solution.py
+++ b/solution.py
@@ -103,7 +103,7 @@
         )
         local = (target - back) / ridge_weight
         stacked = local + dual
-        mean_value = lax.psum(stacked, "tm") / shards
+        mean_value = jnp.sum(lax.all_gather(stacked, "tm"), axis=0) / shards
         norms = jnp.sqrt(jnp.sum(mean_value * mean_value, axis=1))
         level = shrink_level * jnp.mean(norms, axis=1, keepdims=True)
         consensus = shrink_columns(mean_value, norms, level)

time: 316 us -> 269 us (0.85)
  waiting for transfers between devices: 211 us -> 158 us
  other arithmetic: 20.6 us -> 27.7 us
    psum x3 -> x0, waiting for transfers between devices: 157 us -> none  [per_device(): mean_value = lax.psum(stacked, 'tm') / shards]
    all_gather x0 -> x3, waiting for transfers between devices: none -> 103 us  [per_device(): mean_value = jnp.sum(lax.all_gather(stacked, 'tm'), axis=0) / shards]
    reduce_sum x1 -> x3, other arithmetic: 1.9 us -> 9.03 us  [per_device(): mean_value = jnp.sum(lax.all_gather(stacked, 'tm'), axis=0) / shards]
where the time goes in v1:
time: 269 us; the launch traced here: 268 us
  waiting for transfers between devices  158 us (59%)
  other arithmetic  27.7 us (10%)
  blocking collectives  25.2 us (9%)
  matrix products  22.3 us (8%)
  between operations  17.5 us (7%)
  local copies, waits for them, and re-layouts  15.3 us (6%)
    all_gather x3, waiting for transfers between devices, per_device(): mean_value = jnp.sum(lax.all_gather(stacked, 'tm'), axis=0) / shards  103 us
    psum x1, waiting for transfers between devices, per_device(): predicted_output = lax.psum(partial_result, 'boot')  33.1 us
    reduce_scatter x1, waiting for transfers between devices, per_device(): summed = lax.psum_scatter(weighted, 'boot', scatter_dimension=1, tiled=True)  21.9 us
    psum x1, blocking collectives, per_device(): power = lax.psum(jnp.sum(values * values, axis=0), 'tm')  15.2 us
    all_to_all x1, blocking collectives, per_device(): lax.all_to_all(support, 'boot', split_axis=0, concat_axis=1, tiled=True)  10 us
    gather x4, local copies, waits for them, and re-layouts, bootstrap_rows(): jnp.take(window, times + LAGS - 1 - delay_step, axis=0)  9.54 us
    reduce_sum x3, other arithmetic, per_device(): mean_value = jnp.sum(lax.all_gather(stacked, 'tm'), axis=0) / shards  9.03 us
    dot_general x3, matrix products, per_device(): jnp.einsum('brf,bcf->brc', target.astype(jnp.bfloat16), design, preferred...  6.13 us
  transfers between devices with their start and end apart: 6, of which 5 were waited for; matrix products, arithmetic and copies ran while one was open for 1% of the time, Pallas kernels for 0%

profile of v1, /device:TPU:0, one launch (start us, length us, event | category | flops | bytes accessed | tf_op | source)
XLA Modules:
  0.0 267.9 jit_solution(12484436035894477531)
XLA Ops:
  7.2 1.5 copy.24
  9.0 15.2 %psum.14 = f32[1024]{0:T(1024)S(1)} all-reduce(f32[1024]{0:T(1024)S(1)} %fusion.6), channel_id=1, replica_groups=mesh['boot'=4,'tm'=8] {'tm'}, use_global_device_ids=true, to_apply=%region_5.6 | all-reduce | flops 1024 | bytes 8192 | tf_op jit(solution)/shard_map/psum | solution.py:73
  24.6 1.3 collective-permute-start
  26.1 0.6 slice.12
  26.9 0.7 and_reduce_fusion.3
  27.6 0.7 iota_compare_fusion
  28.3 0.7 fusion.109
  29.1 0.7 pad_maximum_fusion
  29.8 0.6 copy.26
  30.4 2.7 %gather_fusion.1 = bf16[384,1024]{1,0:T(8,128)(2,1)} fusion(bf16[516,1024]{1,0:T(8,128)(2,1)S(1)} %copy.26, s32[1024]{0:T(1024)S(1)} %pad_clamp_fusion.3), kind=kCustom, calls=%fused_computation.clone | custom fusion | bytes 1574400 | tf_op jit(solution)/shard_map/vmap(jit(_take))/gather | solution.py:36
  33.1 2.7 %gather_fusion.2 = bf16[384,1024]{1,0:T(8,128)(2,1)} fusion(bf16[516,1024]{1,0:T(8,128)(2,1)S(1)} %copy.26, s32[1024]{0:T(1024)S(1)} %pad_clamp_fusion.2), kind=kCustom, calls=%fused_computation.1.clone | custom fusion | bytes 1574400 | tf_op jit(solution)/shard_map/vmap(jit(_take))/gather | solution.py:36
  35.8 2.1 gather_fusion.4
  37.9 2.1 gather_fusion.3
  40.0 2.8 %fusion.36 = (bf16[1,384,1,1,1,1,1024]{6,1,5,4,3,2,0:T(8,128)(2,1)S(1)}, bf16[384,1024]{1,0:T(8,128)(2,1)}, bf16[384,1024]{1,0:T(8,128)(2,1)}, bf16[1,384,1,1,1,1,1024]{6,1,5,4,3,2,0:T(8,128)(2,1)S(1)}) fusion(bf16[384,1024]{1,0:T(8,128)(2,1)} %gather_fusion.1, pred[384]{0:T(512)(128)(4,1)S(1)} %get-tuple-element.5, bf16[384,1024]{1,0:T(8,128)(2,1)} %gather_fusion.2, ...), kind=kLoop, calls=%fused_computation.80 | loop fusion | flops 786432 | bytes 4719360 | tf_op jit(solution)/shard_map/vmap()/concatenate | solution.py:37
  42.8 1.4 fusion.40
  44.2 0.9 fusion.5
  45.1 3.2 %multiply_reduce_fusion = (f32[]{:T(128)}, f32[384,384]{1,0:T(8,128)}) fusion(bf16[384,4096]{1,0:T(8,128)(2,1)S(1)} %fusion.5), kind=kOutput, calls=%fused_computation.72 | convolution fusion | flops 1208401920 | bytes 3735556 | tf_op jit(solution)/shard_map/bcf,bdf->bcd/dot_general | solution.py:84
  49.4 1.5 fusion.69
  50.9 0.9 copy.25
  51.8 1.9 gather_fusion
  53.7 1.8 convolution_multiply_fusion
  55.6 0.9 maximum_select_fusion.1
  56.5 1.0 convolution_multiply_fusion.4
  59.3 1.5 fusion.2
  61.0 40.0 %all-gather.7.cloned.1.call-done = f32[256,4096]{1,0:T(8,128)} async-done(((f32[32,4096]{1,0:T(8,128)}), f32[256,4096]{1,0:T(8,128)}) %all-gather.7.cloned.1.call-update) | async-done | bytes 4194320 | tf_op jit(solution)/shard_map/all_gather | solution.py:106
  101.0 3.3 %reduce.20 = f32[32,4096]{1,0:T(8,128)} reduce(f32[8,32,4096]{2,1,0:T(8,128)} %bitcast.97, f32[]{:T(128)} %constant.108.clone.1), dimensions={0}, to_apply=%region_7.9 | reduce | flops 917504 | bytes 4718596 | tf_op jit(solution)/shard_map/reduce_sum | solution.py:106
  104.3 1.1 multiply_reduce_fusion.3
  105.4 0.6 sqrt_reduce_fusion.2
  106.7 2.5 convolution_multiply_fusion.3
  110.6 0.5 fusion.30
  111.1 1.5 fusion.3
  112.7 36.7 %all-gather.9.cloned.1.call-done = f32[256,4096]{1,0:T(8,128)} async-done(((f32[32,4096]{1,0:T(8,128)}), f32[256,4096]{1,0:T(8,128)}) %all-gather.9.cloned.1.call-update) | async-done | bytes 4194320 | tf_op jit(solution)/shard_map/all_gather | solution.py:106
  149.4 3.3 %reduce.21 = f32[32,4096]{1,0:T(8,128)} reduce(f32[8,32,4096]{2,1,0:T(8,128)} %bitcast.98, f32[]{:T(128)} %constant.108.clone.1), dimensions={0}, to_apply=%region_10.12 | reduce | flops 917504 | bytes 4718596 | tf_op jit(solution)/shard_map/reduce_sum | solution.py:106
  152.6 1.1 multiply_reduce_fusion.2
  153.7 0.6 sqrt_reduce_fusion.1
  155.1 2.5 convolution_multiply_fusion.2
  159.0 0.5 fusion.31
  159.5 1.5 fusion.4
  161.1 10.0 %all_to_all.13 = s32[4,1,1024]{2,1,0:T(1,128)S(1)} all-to-all(s32[4,1,1024]{2,1,0:T(1,128)S(1)} %all_to_all.10), channel_id=1, replica_groups=mesh['boot'=4,'tm'=8] {'boot'}, dimensions={0} | all-to-all | bytes 32768 | tf_op jit(solution)/shard_map/all_to_all | solution.py:115
  171.1 26.6 %all-gather.11.cloned.1.call-done = f32[256,4096]{1,0:T(8,128)} async-done(((f32[32,4096]{1,0:T(8,128)}), f32[256,4096]{1,0:T(8,128)}) %all-gather.11.cloned.1.call-update) | async-done | bytes 4194320 | tf_op jit(solution)/shard_map/all_gather | solution.py:106
  197.7 2.5 reduce.22
  200.4 0.6 sqrt_reduce_fusion
  201.7 0.8 multiply_multiply_fusion
  202.6 21.9 %reduce-scatter.2.cloned.1.call-done = f32[32,1024]{1,0:T(8,128)} async-done(((f32[32,4096]{1,0:T(8,128)}), f32[32,1024]{1,0:T(8,128)}) %reduce-scatter.2.cloned.1.call-update) | async-done | bytes 131088 | tf_op jit(solution)/shard_map/reduce_scatter | solution.py:119
  224.5 0.9 broadcast_divide_fusion
  225.4 1.3 fusion.33
  226.7 33.1 %all-reduce.2.cloned.1.call-done = f32[32,512]{1,0:T(8,128)} async-done(((f32[32,512]{1,0:T(8,128)}), f32[32,512]{1,0:T(8,128)}) %all-reduce.2.cloned.1.call-update) | async-done | bytes 65552 | tf_op jit(solution)/shard_map/psum | solution.py:131
  259.9 1.5 bitcast_subtract_fusion
  (84 shorter events, 6.2 us)
Async XLA Ops:
  7.2 18.8 %copy-start.19 = (s32[1,6]{1,0:T(1,128)S(1)}, s32[1,6]{1,0:T(1,128)}, u32[]{:S(2)}) copy-start(s32[1,6]{1,0:T(1,128)} %param.8) | copy-start | bytes 76
  7.2 19.6 %copy-start.18 = (s32[1,6]{1,0:T(1,128)S(1)}, s32[1,6]{1,0:T(1,128)}, u32[]{:S(2)}) copy-start(s32[1,6]{1,0:T(1,128)} %param.7) | copy-start | bytes 76
  7.2 93.8 %all-gather.7.cloned.1.call-start = ((), (), s32[]{:S(2)}) async-start(), calls=%async_computation.4 | async-start | bytes 4718592 | tf_op jit(solution)/shard_map/all_gather | solution.py:106
  24.5 4.6 %copy-start.6 = (bf16[512,1024]{0,1:T(8,128)(2,1)}, bf16[512,1024]{0,1:T(8,128)(2,1)S(1)}, u32[]{:S(2)}) copy-start(bf16[512,1024]{0,1:T(8,128)(2,1)S(1)} %fusion.7) | copy-start | bytes 3145732
  24.6 4.4 %collective-permute-start = (bf16[4,1024]{0,1:T(8,128)(2,1)S(1)}, bf16[4,1024]{0,1:T(8,128)(2,1)S(1)}, u32[]{:S(2)}, u32[]{:S(2)}) collective-permute-start(bf16[4,1024]{0,1:T(8,128)(2,1)S(1)} %slice.26), channel_id=1, source_target_pairs={{0,1},{1,2},{2,3},{3,4},{4,5},{5,6},{6,7},{8,9},{9,10},{10,11},{11... | collective-permute-start | bytes 24584 | tf_op jit(solution)/shard_map/ppermute | solution.py:21
  53.7 1.8 copy-start.12
  53.7 1.8 copy-start.13
  53.7 1.9 copy-start.14
  53.7 1.9 copy-start.15
  55.5 3.8 %copy-start.3 = (f32[32,4096]{1,0:T(8,128)}, f32[32,4096]{1,0:T(8,128)S(1)}, u32[]{:S(2)}) copy-start(f32[32,4096]{1,0:T(8,128)S(1)} %convolution_multiply_fusion) | copy-start | bytes 1572868
  56.5 1.1 copy-start
  60.8 88.5 %all-gather.9.cloned.1.call-start = ((), (), s32[]{:S(2)}) async-start(), calls=%async_computation.5 | async-start | bytes 4718592 | tf_op jit(solution)/shard_map/all_gather | solution.py:106
  106.6 2.6 copy-start.1
  106.7 4.4 %copy-start.4 = (f32[32,4096]{1,0:T(8,128)S(1)}, f32[32,4096]{1,0:T(8,128)}, u32[]{:S(2)}) copy-start(f32[32,4096]{1,0:T(8,128)} %copy-done.3) | copy-start | bytes 1572868
  106.7 4.4 %copy-start.10 = (f32[32,4096]{1,0:T(8,128)S(1)}, f32[32,4096]{1,0:T(8,128)}, u32[]{:S(2)}) copy-start(f32[32,4096]{1,0:T(8,128)} %reduce.20) | copy-start | bytes 1572868
  106.7 4.4 %copy-start.11 = (f32[32,4096]{1,0:T(8,128)S(1)}, f32[32,4096]{1,0:T(8,128)}, u32[]{:S(2)}) copy-start(f32[32,4096]{1,0:T(8,128)} %fusion.2) | copy-start | bytes 1572868
  112.6 85.1 %all-gather.11.cloned.1.call-start = ((), (), s32[]{:S(2)}) async-start(), calls=%async_computation.6 | async-start | bytes 4718592 | tf_op jit(solution)/shard_map/all_gather | solution.py:106
  155.0 2.6 copy-start.2
  155.0 4.4 %copy-start.5 = (f32[32,4096]{1,0:T(8,128)S(1)}, f32[32,4096]{1,0:T(8,128)}, u32[]{:S(2)}) copy-start(f32[32,4096]{1,0:T(8,128)} %copy-done.3) | copy-start | bytes 1572868
  155.1 4.4 %copy-start.8 = (f32[32,4096]{1,0:T(8,128)S(1)}, f32[32,4096]{1,0:T(8,128)}, u32[]{:S(2)}) copy-start(f32[32,4096]{1,0:T(8,128)} %fusion.3) | copy-start | bytes 1572868
  155.1 4.4 %copy-start.9 = (f32[32,4096]{1,0:T(8,128)S(1)}, f32[32,4096]{1,0:T(8,128)}, u32[]{:S(2)}) copy-start(f32[32,4096]{1,0:T(8,128)} %reduce.21) | copy-start | bytes 1572868
  159.0 2.1 copy-start.17
  161.0 63.5 %reduce-scatter.2.cloned.1.call-start = ((), (), s32[]{:S(2)}) async-start(), calls=%async_computation.2 | async-start | bytes 655360 | tf_op jit(solution)/shard_map/reduce_scatter | solution.py:119
  197.7 27.7 %copy-start.7 = (bf16[512,1024]{0,1:T(8,128)(2,1)S(1)}, bf16[512,1024]{0,1:T(8,128)(2,1)}, u32[]{:S(2)}) copy-start(bf16[512,1024]{0,1:T(8,128)(2,1)} %copy-done.6) | copy-start | bytes 3145732
  202.5 57.3 %all-reduce.2.cloned.1.call-start = ((), (), s32[]{:S(2)}) async-start(), calls=%async_computation.3 | async-start | bytes 131072 | tf_op jit(solution)/shard_map/psum | solution.py:131
  225.4 35.9 %copy-start.16 = (f32[32,1024]{1,0:T(8,128)}, f32[32,1024]{1,0:T(8,128)S(1)}, u32[]{:S(2)}) copy-start(f32[32,1024]{1,0:T(8,128)S(1)} %broadcast_divide_fusion) | copy-start | bytes 393220
Sparse Core Ops, SparseCore 0:
  60.9 40.0 all-gather.6
  112.8 36.5 all-gather.8
  161.1 36.5 all-gather.10
  202.6 21.8 reduce-scatter.1
  227.2 32.5 all-reduce.1
